TPU v7x, 32 devices: a whole 2x2x4 slice. The times are simulated.
32 devices in a mesh: tok: 8 (over z, x), head: 4 (over y, core).
Axes of the slice: x: 2, y: 2, z: 4, core: 2. Of those that a mesh axis runs over, the one named last changes fastest.
Arguments:
- single: bfloat16 [256, 768], P('tok'), may hold values from -6 to 6
- pair: bfloat16 [256, 256, 128], P('tok', 'head'), may hold values from -161 to 161
- atoms: bfloat16 [6144, 128], P('tok'), may hold values from -60 to 60
- atom_counts: int32 [256], P('tok'), may hold values from 4 to 24, as said below
- w_atom: bfloat16 [128, 3, 128], P(None, None, 'head'), may hold values from -0.5 to 0.5
- w_atom_token: bfloat16 [128, 768], P('head'), may hold values from -6 to 6
- ln_gain: bfloat16 [768], replicated, may hold values from 0.099609375 to 1.8984375
- w_proj: bfloat16 [768, 4, 768], P(None, None, 'head'), may hold values from -0.21875 to 0.21875
- w_pair_bias: bfloat16 [128, 16], replicated, may hold values from -3.5 to 3.5
- w_out: bfloat16 [768, 768], P('head'), may hold values from -0.21875 to 0.21875
- ln_gain2: bfloat16 [768], replicated, may hold values from 0.099609375 to 1.8984375
- w_trans: bfloat16 [768, 2, 1536], P(None, None, 'head'), may hold values from -0.21875 to 0.21875
- w_trans_out: bfloat16 [1536, 768], P('head'), may hold values from -0.15625 to 0.15625
Outputs:
- refined: bfloat16 [256, 768], P('tok', 'head')
- atom_mix: bfloat16 [128, 6144], P('head', 'tok')
Inputs may be any that keep to these rules, and one draw needn't show every extreme that they name: `atom_counts`: every token has 4 to 24 atoms; in every draw all tokens of some group of 32 have 24 atoms.
All inputs are finite; a program needn't handle non-finite values.
Results may differ from a plain program's by a relative error of at most 0.013.
Values may be sent and summed in bfloat16 or wider, within the bound.
A program may use at most 64 MiB of HBM per device.

v0:
```python
import functools

import jax
import jax.numpy as jnp
from jax import lax
from jax.experimental import pallas as pl
from jax.experimental.pallas import tpu as pltpu
from jax.sharding import PartitionSpec as P

H = 16
AH = 4
QWIN = 32
KWIN = 128
TAIL = (KWIN - QWIN) // 2
LEAD = (KWIN + QWIN) // 2
MESH = pl.DeviceIdType.MESH
f32 = jnp.float32
bf16 = jnp.bfloat16

norm_eps = 1e-05
masked_value = -1000000000.0
GROUP = 4
VMEM_MIB = 58


def dot(a, b):
    return jnp.dot(a, b, preferred_element_type=f32)


def dot_t(a, b):
    return lax.dot_general(a, b, (((1,), (1,)), ((), ())), preferred_element_type=f32)


def iota(shape, dim):
    return lax.broadcasted_iota(jnp.int32, shape, dim)


def eye(n):
    return (iota((n, n), 0) == iota((n, n), 1)).astype(bf16)


def layer_norm(x, gain):
    average = jnp.mean(x, axis=-1, keepdims=True)
    centred = x - average
    spread = jnp.mean(centred * centred, axis=-1, keepdims=True)
    return centred * lax.rsqrt(spread + norm_eps) * gain.astype(f32)


def kernel(
    nt,
    nh,
    single_hbm,
    pair_hbm,
    atoms_hbm,
    counts,
    w_atom_hbm,
    w_tok_hbm,
    gain1,
    w_proj_hbm,
    w_pair_hbm,
    w_out_hbm,
    gain2,
    w_trans_hbm,
    w_down_hbm,
    refined,
    atom_mix,
    single,
    atoms,
    w_atom,
    w_tok,
    w_pair,
    pair,
    w_proj,
    w_out,
    w_trans,
    w_down,
    local_sem,
    tail,
    halo_prev,
    halo_next,
    halo_s,
    halo_r,
    sg,
    sg_s,
    sg_r,
    fwd_s,
    fwd_r,
    wt,
    wt_s,
    wt_r,
    pair_f,
    pair_s,
    pair_r,
    pb_s,
    pb_r,
    keys,
    values,
    ta,
    ta_s,
    ta_r,
    parts,
    part_s,
    part_r,
    fin_s_buf,
    fin_r_buf,
    own_buf,
    fin_s,
    fin_r,
):
    t = lax.axis_index("tok")
    h = lax.axis_index("head")
    n = nt * nh
    me = t * nh + h
    rows, width = single.shape
    slots = atoms.shape[0]
    awidth = w_atom.shape[1]
    heads = w_pair.shape[0]
    local_heads = heads // nh
    lw = w_proj.shape[1]
    hd = lw // local_heads
    kblock = pair.shape[1]
    half = width // 2

    locals_ = [
        pltpu.make_async_copy(src, dst, local_sem.at[i])
        for i, (src, dst) in enumerate(
            [
                (atoms_hbm, atoms),
                (single_hbm, single),
                (w_tok_hbm, w_tok),
                (w_atom_hbm, w_atom),
                (w_pair_hbm, w_pair),
                (pair_hbm, pair),
                (w_proj_hbm, w_proj),
                (w_out_hbm, w_out),
                (w_trans_hbm, w_trans),
                (w_down_hbm, w_down),
            ]
        )
    ]
    for copy in locals_:
        copy.start()

    barrier = pltpu.get_barrier_semaphore()

    def greet(o, c):
        peer = lax.rem(me + o, n)
        pl.semaphore_signal(
            barrier, inc=1, device_id=(lax.div(peer, nh), lax.rem(peer, nh)), device_id_type=MESH
        )
        return c

    lax.fori_loop(1, n, greet, 0)

    cnt_row = counts[...].astype(f32)
    ri = iota((rows, rows), 0)
    ci = iota((rows, rows), 1)
    cnt_b = jnp.broadcast_to(cnt_row, (rows, rows))
    cnt_col = jnp.sum(jnp.where(ri == ci, cnt_b, 0.0), axis=1, keepdims=True)
    end_col = jnp.sum(jnp.where(ci <= ri, cnt_b, 0.0), axis=1, keepdims=True)
    live = jnp.sum(cnt_row, axis=1, keepdims=True).astype(jnp.int32)
    end_i = end_col.astype(jnp.int32)
    start_i = (end_col - cnt_col).astype(jnp.int32)

    locals_[0].wait()
    pick = iota((TAIL, slots), 1) == iota((TAIL, slots), 0) + (live - TAIL)
    tail[...] = dot(pick.astype(bf16), atoms[...]).astype(bf16)

    c_half = lax.rem(h, 2)
    locals_[1].wait()
    locals_[2].wait()
    sg[c_half, pl.ds(pl.multiple_of(t * rows, rows), rows), :] = single[
        :, pl.ds(pl.multiple_of(c_half * half, 128), half)
    ]
    wt[h] = w_tok[...]

    locals_[3].wait()
    alive = iota((slots, 1), 0) < live
    place = (iota((slots + LEAD, LEAD), 0) - live == iota((slots + LEAD, LEAD), 1)).astype(bf16)
    queries = dot_t(atoms[...], w_atom[0]).astype(bf16)
    own_kv = [dot_t(atoms[...], w_atom[i]) for i in (1, 2)]
    kv = (keys, values)
    for ref, x in zip(kv, own_kv):
        ref[TAIL : TAIL + slots, :awidth] = x.astype(bf16)
    values[:, awidth:] = jnp.ones((values.shape[0], awidth), bf16)

    pl.semaphore_wait(barrier, n - 1)

    nxt = lax.rem(t + 1, nt)
    prv = lax.rem(t + nt - 1, nt)
    up = pltpu.make_async_remote_copy(
        tail, halo_prev, halo_s.at[0], halo_r.at[0], device_id=(nxt, h), device_id_type=MESH
    )
    down = pltpu.make_async_remote_copy(
        atoms.at[pl.ds(0, LEAD)], halo_next, halo_s.at[1], halo_r.at[1], device_id=(prv, h), device_id_type=MESH
    )
    up.start()
    down.start()

    def head_copies(src_of, dst, s, r):
        out = []
        for o in range(1, nh):
            peer = lax.rem(h + o, nh)
            out.append(
                pltpu.make_async_remote_copy(
                    src_of(peer), dst.at[h], s.at[o], r.at[o], device_id=(t, peer), device_id_type=MESH
                )
            )
        return out

    def sg_copy(o):
        peer = lax.rem(t + o, nt)
        block = sg.at[c_half, pl.ds(pl.multiple_of(t * rows, rows), rows), :]
        return pltpu.make_async_remote_copy(
            block, block, sg_s.at[o], sg_r.at[o], device_id=(peer, h), device_id_type=MESH
        )

    def start_sg(o, c):
        sg_copy(o).start()
        return c

    lax.fori_loop(1, nt, start_sg, 0)
    wt_copies = head_copies(lambda peer: wt.at[h], wt, wt_s, wt_r)
    for copy in wt_copies:
        copy.start()

    locals_[4].wait()
    locals_[5].wait()
    for i in range(rows):
        pair_f[:, i, :] = dot_t(w_pair[...], pair[i])
    for p in range(nh):
        pair_s[p] = pair_f[p * local_heads : (p + 1) * local_heads].astype(bf16)
    pair_r[h] = pair_s[h]
    pb_copies = head_copies(lambda peer: pair_s.at[peer], pair_r, pb_s, pb_r)
    for copy in pb_copies:
        copy.start()

    up.wait()
    down.wait()
    for ref, i in ((keys, 1), (values, 2)):
        ref[0:TAIL, :awidth] = dot_t(halo_prev[...], w_atom[i]).astype(bf16)
        placed = dot(place, dot_t(halo_next[...], w_atom[i]).astype(bf16)).astype(bf16)
        ref[TAIL : TAIL + slots, :awidth] = jnp.where(alive, ref[TAIL : TAIL + slots, :awidth], placed[:slots])
        ref[TAIL + slots : TAIL + slots + LEAD, :awidth] = placed[slots:]

    low = jnp.where(t > 0, -KWIN, 0)
    high = jnp.where(t < nt - 1, slots + 2 * KWIN, live)
    scale = awidth ** (-0.5)
    qrows = GROUP * QWIN
    krows = qrows + KWIN
    lane = iota((1, krows), 1)
    first = iota((qrows, krows), 0) // QWIN * QWIN
    lanes = iota((qrows, krows), 1)
    band = jnp.where((lanes >= first) & (lanes < first + KWIN), 0.0, masked_value)
    mixed = []
    groups = slots // qrows
    for w in range(groups):
        if w == groups // 2:

            def wait_sg(o, c):
                sg_copy(o).wait_recv()
                return c

            lax.fori_loop(1, nt, wait_sg, 0)
            partner = h + 1 - 2 * c_half
            fwd = pltpu.make_async_remote_copy(
                sg.at[c_half], sg.at[c_half], fwd_s, fwd_r, device_id=(t, partner), device_id_type=MESH
            )
            fwd.start()
        a = w * qrows
        pos = lane + (a - TAIL)
        outside = jnp.where((pos >= low) & (pos < high), 0.0, masked_value)
        s = dot_t(queries[a : a + qrows], keys[a : a + krows, :]) * scale + (band + outside)
        e = jnp.exp(s - jnp.max(s, axis=-1, keepdims=True)).astype(bf16)
        pv = dot(e, values[a : a + krows, :])
        mixed.append(pv[:, :awidth] / pv[:, awidth : awidth + 1])
    mix = jnp.where(alive, jnp.concatenate(mixed, axis=0), 0.0).astype(bf16)
    slot = iota((rows, slots), 1)
    member = ((slot >= start_i) & (slot < end_i)).astype(bf16)
    means = dot(member, mix) / cnt_col
    packs = KWIN // awidth
    prow = rows // packs
    packed = jnp.concatenate([means[i * prow : (i + 1) * prow] for i in range(packs)], axis=1)
    ta[h, t] = packed.astype(bf16)

    def ta_copy(o):
        peer = lax.rem(me + o, n)
        block = ta.at[h, t]
        return pltpu.make_async_remote_copy(
            block,
            block,
            ta_s.at[o],
            ta_r.at[o],
            device_id=(lax.div(peer, nh), lax.rem(peer, nh)),
            device_id_type=MESH,
        )

    def start_ta(o, c):
        ta_copy(o).start()
        return c

    lax.fori_loop(1, n, start_ta, 0)
    atom_mix[...] = dot_t(eye(awidth), mix).astype(bf16)

    fwd.wait_recv()
    for copy in wt_copies:
        copy.wait_recv()
    locals_[6].wait()

    def wait_ta(o, c):
        ta_copy(o).wait_recv()
        return c

    lax.fori_loop(1, n, wait_ta, 0)

    own = single[...].astype(f32)
    full = jnp.concatenate([sg[0], sg[1]], axis=1).astype(f32)
    at_lane = iota((1, packs * awidth), 1)

    def spread(x):
        x = x.astype(f32)
        return [
            jnp.where((at_lane >= i * awidth) & (at_lane < (i + 1) * awidth), x, 0.0)
            for i in range(packs)
        ]

    lhs = jnp.concatenate(
        [
            jnp.concatenate([m.reshape(nt, 1, prow, packs * awidth) for m in spread(ta[p].astype(f32).reshape(nt * prow, packs * awidth))], axis=1)
            .reshape(nt * rows, packs * awidth)
            .astype(bf16)
            for p in range(nh)
        ],
        axis=1,
    )
    own_lhs = jnp.concatenate(
        [jnp.concatenate(spread(ta[p, t]), axis=0).astype(bf16) for p in range(nh)], axis=1
    )
    wide = jnp.concatenate([wt[p] for p in range(nh) for i in range(packs)], axis=0)
    term = dot(lhs, wide)
    own_term = dot(own_lhs, wide)
    state = own + own_term
    normed_own = layer_norm(state, gain1[...].reshape(1, width)).astype(bf16)
    normed = layer_norm(full + term, gain1[...].reshape(1, width)).astype(bf16)
    q = dot_t(normed_own, w_proj[0])
    k = dot_t(normed, w_proj[1]).astype(bf16)
    v = dot_t(normed, w_proj[2]).astype(bf16)
    gate = jax.nn.sigmoid(dot_t(normed_own, w_proj[3]))
    col = iota((1, lw), 1)
    in_head = [(col >= hd * i) & (col < hd * (i + 1)) for i in range(local_heads)]
    stacked = jnp.concatenate([jnp.where(m, q, 0.0) for m in in_head], axis=0).astype(bf16)
    s = dot_t(stacked, k) * hd ** (-0.5)
    for copy in pb_copies:
        copy.wait_recv()
    bias = jnp.concatenate(
        [pair_r[p].astype(f32).reshape(local_heads * rows, kblock) for p in range(nh)], axis=1
    )
    s = s + bias
    e = jnp.exp(s - jnp.max(s, axis=-1, keepdims=True))
    p_ = (e / jnp.sum(e, axis=-1, keepdims=True)).astype(bf16)
    ctx = dot(p_, v)
    context = jnp.zeros((rows, lw), f32)
    for i, m in enumerate(in_head):
        context = jnp.where(m, ctx[i * rows : (i + 1) * rows], context)
    gated = (context * gate).astype(bf16)
    locals_[7].wait()
    parts[h] = dot(gated, w_out[...]).astype(bf16)
    part_copies = head_copies(lambda peer: parts.at[h], parts, part_s, part_r)
    for copy in part_copies:
        copy.start()
    locals_[8].wait()
    locals_[9].wait()
    for copy in part_copies:
        copy.wait_recv()
    total = parts[0].astype(f32)
    for p in range(1, nh):
        total += parts[p].astype(f32)
    after = state + total
    normed_after = layer_norm(after, gain2[...].reshape(1, width)).astype(bf16)
    g = dot(normed_after, w_trans[0])
    u = dot(normed_after, w_trans[1])
    hidden = (jax.nn.silu(g) * u).astype(bf16)
    update = dot(hidden, w_down[...])
    quarter = width // nh
    for p in range(nh):
        fin_s_buf[p] = update[:, p * quarter : (p + 1) * quarter].astype(bf16)
        own_buf[p] = after[:, p * quarter : (p + 1) * quarter]
    fin_copies = head_copies(lambda peer: fin_s_buf.at[peer], fin_r_buf, fin_s, fin_r)
    for copy in fin_copies:
        copy.start()
    acc = own_buf[h] + fin_s_buf[h].astype(f32)
    fin_r_buf[h] = jnp.zeros((rows, quarter), bf16)

    up_down_done = wt_copies + pb_copies + part_copies
    for copy in up_down_done:
        copy.wait_send()
    fwd.wait_send()

    def drain_sg(o, c):
        sg_copy(o).wait_send()
        return c

    def drain_ta(o, c):
        ta_copy(o).wait_send()
        return c

    lax.fori_loop(1, nt, drain_sg, 0)
    lax.fori_loop(1, n, drain_ta, 0)
    for copy in fin_copies:
        copy.wait()
    for p in range(nh):
        acc += fin_r_buf[p].astype(f32)
    refined[...] = acc.astype(bf16)


def shards(
    nt,
    nh,
    single,
    pair,
    atoms,
    atom_counts,
    w_atom,
    w_atom_token,
    ln_gain,
    w_proj,
    w_pair_bias,
    w_out,
    ln_gain2,
    w_trans,
    w_trans_out,
):
    rows, width = single.shape
    slots, channels = atoms.shape
    awidth = w_atom.shape[2]
    heads = w_pair_bias.shape[1]
    local_heads = heads // nh
    kblock = pair.shape[1]
    n = nt * nh
    lw = w_proj.shape[2]
    hidden = w_trans.shape[2]
    quarter = width // nh
    vm = pl.BlockSpec(memory_space=pltpu.VMEM)
    hbm = pl.BlockSpec(memory_space=pltpu.HBM)
    anywhere = pl.BlockSpec(memory_space=pl.ANY)
    dma = pltpu.SemaphoreType.DMA
    return pl.pallas_call(
        functools.partial(kernel, nt, nh),
        out_shape=(
            jax.ShapeDtypeStruct((rows, quarter), bf16),
            jax.ShapeDtypeStruct((awidth, slots), bf16),
        ),
        in_specs=[hbm, hbm, hbm, vm, hbm, hbm, vm, hbm, hbm, hbm, vm, anywhere, hbm],
        out_specs=(vm, vm),
        scratch_shapes=[
            pltpu.VMEM(single.shape, bf16),
            pltpu.VMEM(atoms.shape, bf16),
            pltpu.VMEM((3, awidth, channels), bf16),
            pltpu.VMEM(w_atom_token.shape, bf16),
            pltpu.VMEM((heads, pair.shape[2]), bf16),
            pltpu.VMEM(pair.shape, bf16),
            pltpu.VMEM((4, lw, width), bf16),
            pltpu.VMEM(w_out.shape, bf16),
            pltpu.VMEM((2, width, hidden), bf16),
            pltpu.VMEM(w_trans_out.shape, bf16),
            dma((10,)),
            pltpu.VMEM((TAIL, channels), bf16),
            pltpu.VMEM((TAIL, channels), bf16),
            pltpu.VMEM((LEAD, channels), bf16),
            dma((2,)),
            dma((2,)),
            pltpu.VMEM((2, nt * rows, width // 2), bf16),
            dma((nt,)),
            dma((nt,)),
            dma,
            dma,
            pltpu.VMEM((nh, awidth, width), bf16),
            dma((nh,)),
            dma((nh,)),
            pltpu.VMEM((heads, rows, kblock), f32),
            pltpu.VMEM((nh, local_heads, rows, kblock), bf16),
            pltpu.VMEM((nh, local_heads, rows, kblock), bf16),
            dma((nh,)),
            dma((nh,)),
            pltpu.VMEM((TAIL + slots + LEAD, awidth), bf16),
            pltpu.VMEM((TAIL + slots + LEAD, 2 * awidth), bf16),
            pltpu.VMEM((nh, nt, rows * awidth // KWIN, KWIN), bf16),
            dma((n,)),
            dma((n,)),
            pltpu.VMEM((nh, rows, width), bf16),
            dma((nh,)),
            dma((nh,)),
            pltpu.VMEM((nh, rows, quarter), bf16),
            pltpu.VMEM((nh, rows, quarter), bf16),
            pltpu.VMEM((nh, rows, quarter), f32),
            dma((nh,)),
            dma((nh,)),
        ],
        compiler_params=pltpu.CompilerParams(
            collective_id=0, has_side_effects=True, vmem_limit_bytes=VMEM_MIB * 1024 * 1024
        ),
        name="step",
    )(
        single,
        pair,
        atoms,
        atom_counts.reshape(1, rows),
        jnp.transpose(w_atom, (1, 2, 0)),
        w_atom_token,
        ln_gain,
        jnp.transpose(w_proj, (1, 2, 0)),
        w_pair_bias.T,
        w_out,
        ln_gain2,
        jnp.transpose(w_trans, (1, 0, 2)),
        w_trans_out,
    )


def solution(mesh):
    return jax.shard_map(
        functools.partial(shards, mesh.shape["tok"], mesh.shape["head"]),
        mesh=mesh,
        in_specs=(
            P("tok", None),
            P("tok", "head", None),
            P("tok", None),
            P("tok"),
            P(None, None, "head"),
            P("head", None),
            P(),
            P(None, None, "head"),
            P(),
            P("head", None),
            P(),
            P(None, None, "head"),
            P("head", None),
        ),
        out_specs=(P("tok", "head"), P("head", "tok")),
        check_vma=False,
    )
```

profile of v0, /device:TPU:0, one launch (start us, length us, event | category | flops | bytes accessed | tf_op | source)
XLA Modules:
  0.0 36.1 jit_solution(9339586885824454993)
XLA Ops:
  0.6 2.4 %copy.17 = bf16[768,2,384]{2,0,1:T(8,128)(2,1)} copy(bf16[768,2,384]{2,1,0:T(2,128)(2,1)} %param.24) | data formatting | bytes 2359296 | tf_op args[11]
  3.1 30.3 %step.1 = (bf16[32,192]{1,0:T(8,128)(2,1)}, bf16[32,768]{1,0:T(8,128)(2,1)}) custom-call(bf16[32,768]{1,0:T(8,128)(2,1)} %single_hbm.1, bf16[32,64,128]{2,1,0:T(8,128)(2,1)} %pair_hbm.1, bf16[768,128]{1,0:T(8,128)(2,1)} %atoms_hbm.1, s32[1,32]{1,0:T(1,128)} %bitcast.11, bf16[3,32,128]{2,1,0:T(8,128)(2,1)} %bitcast.9, bf16[32,768]{1,0:T(8,128)(2,1)} %w_tok_hbm.1, ...), custom_call_target="tpu_custom_call" | custom-call | tf_op jit(solution)/shard_map/step/pallas_call | solution.py:447
  33.4 1.3 %copy.20 = bf16[32,192]{1,0:T(8,128)(2,1)} copy(bf16[32,192]{1,0:T(8,128)(2,1)} %get-tuple-element.4) | data formatting | bytes 24576
  34.7 1.4 %copy.21 = bf16[32,768]{1,0:T(8,128)(2,1)} copy(bf16[32,768]{1,0:T(8,128)(2,1)} %get-tuple-element.5) | data formatting | bytes 98304
where the time goes:
time: 36.4 us; the launch traced here: 36.1 us
  Pallas kernels  30.3 us (83%)
  local copies, waits for them, and re-layouts  5.18 us (14%)
  between operations  0.64 us (2%)
    pallas_call x1, Pallas kernels, shards(): pl.pallas_call(functools.partial(kernel, nt, nh), out_shape=(jax.ShapeDty...  30.3 us
    unnamed x3, local copies, waits for them, and re-layouts  5.18 us

commit v1 on v0

v1 whole, which is shorter than its diff:
```python
import functools

import jax
import jax.numpy as jnp
from jax import lax
from jax.experimental import pallas as pl
from jax.experimental.pallas import tpu as pltpu
from jax.sharding import PartitionSpec as P

H = 16
AH = 4
QWIN = 32
KWIN = 128
TAIL = (KWIN - QWIN) // 2
LEAD = (KWIN + QWIN) // 2
MESH = pl.DeviceIdType.MESH
f32 = jnp.float32
bf16 = jnp.bfloat16

norm_eps = 1e-05
masked_value = -1000000000.0
GROUP = 4
FRONT = 2 * QWIN
EDGE = 3
FRONT = 2 * QWIN
EDGE = 3
FRONT = 2 * QWIN
EDGE = 3
FRONT = 2 * QWIN
EDGE = 3
FRONT = 2 * QWIN
EDGE = 3
VMEM_MIB = 58


def dot(a, b):
    return jnp.dot(a, b, preferred_element_type=f32)


def dot_t(a, b):
    return lax.dot_general(a, b, (((1,), (1,)), ((), ())), preferred_element_type=f32)


def iota(shape, dim):
    return lax.broadcasted_iota(jnp.int32, shape, dim)


def eye(n):
    return (iota((n, n), 0) == iota((n, n), 1)).astype(bf16)


def layer_norm(x, gain):
    average = jnp.mean(x, axis=-1, keepdims=True)
    centred = x - average
    spread = jnp.mean(centred * centred, axis=-1, keepdims=True)
    return centred * lax.rsqrt(spread + norm_eps) * gain.astype(f32)


def total_wait(ref, sem):
    pltpu.make_async_copy(ref, ref, sem).wait()


def total_wait(ref, sem):
    pltpu.make_async_copy(ref, ref, sem).wait()


def total_wait(ref, sem):
    pltpu.make_async_copy(ref, ref, sem).wait()


def total_wait(ref, sem):
    pltpu.make_async_copy(ref, ref, sem).wait()


def total_wait(ref, sem):
    pltpu.make_async_copy(ref, ref, sem).wait()


def kernel(
    nt,
    nh,
    single_hbm,
    pair_hbm,
    atoms_hbm,
    counts_hbm,
    w_atom_hbm,
    w_tok_hbm,
    gain1_hbm,
    w_proj_hbm,
    w_pair_hbm,
    w_out_hbm,
    gain2_hbm,
    w_trans_hbm,
    w_down_hbm,
    refined,
    atom_mix,
    counts,
    single,
    atoms,
    w_atom,
    w_tok,
    gain1,
    gain2,
    w_pair,
    pair,
    w_proj,
    w_out,
    w_raw,
    w_gate,
    w_up,
    w_down,
    local_sem,
    tail,
    halo,
    halo_s,
    halo_r,
    sg,
    sg_s,
    sg_r,
    fwd_s,
    fwd_r,
    wt,
    wt_s,
    wt_r,
    pair_f,
    pair_s,
    pair_r,
    pb_s,
    pb_r,
    queries,
    keys,
    values,
    inner,
    mixed,
    ta,
    ta_s,
    ta_r,
    parts,
    part_s,
    part_r,
    fin_s_buf,
    fin_r_buf,
    own_buf,
    fin_s,
    fin_r,
):
    t = lax.axis_index("tok")
    h = lax.axis_index("head")
    rows, width = single.shape
    slots = atoms.shape[0]
    awidth = w_atom.shape[1]
    heads = w_pair.shape[0]
    local_heads = heads // nh
    lw = w_proj.shape[1]
    hd = lw // local_heads
    kblock = pair.shape[1]
    half = width // 2
    hidden_width = w_gate.shape[1]

    barrier = pltpu.get_barrier_semaphore()
    head_peers = [lax.rem(h + o, nh) for o in range(nh)]

    def everyone(act):
        for peer in head_peers[1:]:
            act(t, peer)

        def step(o, c):
            other = lax.rem(t + o, nt)
            for peer in head_peers:
                act(other, peer)
            return c

        lax.fori_loop(1, nt, step, 0)

    everyone(
        lambda pt, ph: pl.semaphore_signal(barrier, inc=1, device_id=(pt, ph), device_id_type=MESH)
    )

    locals_ = [
        pltpu.make_async_copy(src, dst, local_sem.at[i])
        for i, (src, dst) in enumerate(
            [
                (atoms_hbm, atoms),
                (counts_hbm, counts),
                (w_atom_hbm, w_atom),
                (single_hbm, single),
                (w_tok_hbm, w_tok),
                (w_pair_hbm, w_pair),
                (pair_hbm, pair),
                (w_trans_hbm, w_raw),
                (w_proj_hbm, w_proj),
                (gain1_hbm, gain1),
                (w_out_hbm, w_out),
                (gain2_hbm, gain2),
                (w_down_hbm, w_down),
            ]
        )
    ]
    for copy in locals_:
        copy.start()

    locals_[1].wait()
    cnt_row = counts[...].astype(f32)
    live = jnp.sum(cnt_row, axis=1, keepdims=True).astype(jnp.int32)
    locals_[0].wait()

    @pl.when(t < nt - 1)
    def _():
        pick = iota((TAIL, slots), 1) == iota((TAIL, slots), 0) + (live - TAIL)
        tail[...] = dot(pick.astype(bf16), atoms[...]).astype(bf16)

    c_half = lax.rem(h, 2)
    locals_[3].wait()
    locals_[4].wait()
    sg[c_half, pl.ds(pl.multiple_of(t * rows, rows), rows), :] = single[
        :, pl.ds(pl.multiple_of(c_half * half, 128), half)
    ]
    wt[h] = w_tok[...]

    pl.semaphore_wait(barrier, nt * nh - 1)

    nxt = lax.rem(t + 1, nt)
    prv = lax.rem(t + nt - 1, nt)
    up = pltpu.make_async_remote_copy(
        tail, halo.at[pl.ds(0, TAIL)], halo_s.at[0], halo_r.at[0], device_id=(nxt, h), device_id_type=MESH
    )
    down = pltpu.make_async_remote_copy(
        atoms.at[pl.ds(0, LEAD)],
        halo.at[pl.ds(TAIL, LEAD)],
        halo_s.at[1],
        halo_r.at[1],
        device_id=(prv, h),
        device_id_type=MESH,
    )
    down.start()
    up.start()

    def head_send(src_of, dst, s, r):
        for peer in head_peers[1:]:
            pltpu.make_async_remote_copy(
                src_of(peer), dst.at[h], s, r, device_id=(t, peer), device_id_type=MESH
            ).start()

    def head_wait(ref, sem):
        total_wait(ref.at[pl.ds(0, nh - 1)], sem)

    own_rows = pl.ds(pl.multiple_of(t * rows, rows), rows)

    def start_sg(o, c):
        block = sg.at[c_half, own_rows, :]
        pltpu.make_async_remote_copy(
            block, block, sg_s, sg_r, device_id=(lax.rem(t + o, nt), h), device_id_type=MESH
        ).start()
        return c

    lax.fori_loop(1, nt, start_sg, 0)
    head_send(lambda peer: wt.at[h], wt, wt_s, wt_r)

    ri = iota((rows, rows), 0)
    ci = iota((rows, rows), 1)
    cnt_b = jnp.broadcast_to(cnt_row, (rows, rows))
    cnt_col = jnp.sum(jnp.where(ri == ci, cnt_b, 0.0), axis=1, keepdims=True)
    end_col = jnp.sum(jnp.where(ci <= ri, cnt_b, 0.0), axis=1, keepdims=True)
    end_i = end_col.astype(jnp.int32)
    start_i = (end_col - cnt_col).astype(jnp.int32)
    last = (live - 1) // QWIN
    r0 = (last - (EDGE - 1)) * QWIN

    locals_[2].wait()
    queries[...] = dot_t(atoms[...], w_atom[0]).astype(bf16)
    for ref, i in ((keys, 1), (values, 2)):
        ref[TAIL : TAIL + slots, :awidth] = dot_t(atoms[...], w_atom[i]).astype(bf16)
        ref[0:TAIL, :awidth] = jnp.zeros((TAIL, awidth), bf16)
        ref[TAIL + slots :, :awidth] = jnp.zeros((LEAD, awidth), bf16)
    values[:, awidth:] = jnp.ones((values.shape[0], values.shape[1] - awidth), bf16)

    locals_[5].wait()
    locals_[6].wait()
    for i in range(rows):
        pair_f[:, i, :] = dot_t(w_pair[...], pair[i])
    for p in range(nh):
        pair_s[p] = pair_f[p * local_heads : (p + 1) * local_heads].astype(bf16)
    pair_r[h] = pair_s[h]
    head_send(lambda peer: pair_s.at[peer], pair_r, pb_s, pb_r)

    scale = awidth ** (-0.5)
    qrows = GROUP * QWIN
    krows = qrows + KWIN
    lane = iota((1, krows), 1)
    first = iota((qrows, krows), 0) // QWIN * QWIN
    lanes = iota((qrows, krows), 1)
    band = jnp.where((lanes >= first) & (lanes < first + KWIN), 0.0, masked_value)
    wide_lane = iota((qrows, KWIN), 1)
    for w in range(slots // qrows):
        a = w * qrows
        pos = lane + (a - TAIL)
        outside = jnp.where((pos >= 0) & (pos < live), 0.0, masked_value)
        s = dot_t(queries[a : a + qrows], keys[a : a + krows, :]) * scale + (band + outside)
        top = jnp.max(s, axis=-1, keepdims=True)
        e = jnp.exp(s - top).astype(bf16)
        pv = dot(e, values[a : a + krows, :])
        inner[a : a + qrows] = jnp.where(wide_lane < 2 * awidth, pv, top)
        mixed[a : a + qrows] = (pv[:, :awidth] / pv[:, awidth : awidth + 1]).astype(bf16)

    slot = iota((rows, slots), 1)
    member = (slot >= start_i) & (slot < end_i)
    inside = member & (slot >= FRONT) & ((slot < r0) | (slot >= r0 + EDGE * QWIN))
    sums = dot(inside.astype(bf16), mixed[...])
    erow = iota((rows, FRONT + EDGE * QWIN), 1)
    eslot = jnp.where(erow < FRONT, erow, erow - FRONT + r0)
    touched = (eslot >= start_i) & (eslot < end_i) & ((erow < FRONT) | (eslot >= FRONT))
    touched = touched.astype(bf16)

    nrow = FRONT + EDGE * QWIN
    qi = iota((nrow, KWIN), 0)
    ki = iota((nrow, KWIN), 1)
    seen_prev = (qi < FRONT) & (ki < TAIL) & (ki >= qi // QWIN * QWIN) & (t > 0)
    reach = (qi - FRONT) // QWIN * QWIN + r0 + LEAD - live
    seen_next = (qi >= FRONT) & (ki >= TAIL) & (ki - TAIL < reach) & (t < nt - 1)
    edge_mask = jnp.where(seen_prev | seen_next, 0.0, masked_value)
    pick = iota((EDGE * QWIN, slots), 1) == iota((EDGE * QWIN, slots), 0) + r0
    a_edge = dot(pick.astype(bf16), atoms[...]).astype(bf16)
    a_edge = jnp.concatenate([atoms[0:FRONT], a_edge], axis=0)
    q_edge = dot_t(a_edge, w_atom[0]).astype(bf16)
    in_edge = jnp.dot(pick.astype(f32), inner[...], precision=lax.Precision.HIGHEST, preferred_element_type=f32)
    in_edge = jnp.concatenate([inner[0:FRONT], in_edge], axis=0)
    top_in = in_edge[:, 2 * awidth : 2 * awidth + 1]

    locals_[7].wait()
    woven = w_raw[...].reshape(2 * width, hidden_width)
    blk = 128
    si = iota((blk, 2 * blk), 0)
    sj = iota((blk, 2 * blk), 1)
    picks = [(sj == 2 * si + p).astype(bf16) for p in (0, 1)]
    for b in range(width // blk):
        for p, ref in enumerate((w_gate, w_up)):
            ref[b * blk : (b + 1) * blk] = dot(picks[p], woven[2 * b * blk : 2 * (b + 1) * blk]).astype(bf16)

    up.wait_recv()
    down.wait_recv()
    kh = dot_t(halo[...], w_atom[1]).astype(bf16)
    vh = dot_t(halo[...], w_atom[2]).astype(bf16)
    vh = jnp.concatenate([vh, jnp.ones((KWIN, KWIN - awidth), bf16)], axis=1)
    s = dot_t(q_edge, kh) * scale + edge_mask
    top_out = jnp.max(s, axis=-1, keepdims=True)
    e = jnp.exp(s - top_out).astype(bf16)
    pv = dot(e, vh)
    top = jnp.maximum(top_in, top_out)
    pv = jnp.exp(top_in - top) * in_edge + jnp.exp(top_out - top) * pv
    edge = (pv[:, :awidth] / pv[:, awidth : awidth + 1]).astype(bf16)
    means = (sums + dot(touched, edge)) / cnt_col
    packs = KWIN // awidth
    prow = rows // packs
    packed = jnp.concatenate([means[i * prow : (i + 1) * prow] for i in range(packs)], axis=1)
    ta[h, t] = packed.astype(bf16)

    def ta_send(pt, ph):
        block = ta.at[h, t]
        pltpu.make_async_remote_copy(
            block, block, ta_s, ta_r, device_id=(pt, ph), device_id_type=MESH
        ).start()

    everyone(ta_send)

    at_window = iota((QWIN, awidth), 0) // QWIN
    for w in range(slots // QWIN):
        a = w * QWIN
        if a < FRONT:
            mixed[a : a + QWIN] = edge[a : a + QWIN]
        else:
            block = mixed[a : a + QWIN].astype(f32)
            for i in range(EDGE):
                b = FRONT + i * QWIN
                here = at_window + (w + EDGE - 1 - i) == last
                block = jnp.where(here, edge[b : b + QWIN].astype(f32), block)
            mixed[a : a + QWIN] = block.astype(bf16)
    alive = iota((slots, 1), 0) < live
    mix = jnp.where(alive, mixed[...].astype(f32), 0.0).astype(bf16)
    atom_mix[...] = dot_t(eye(awidth), mix).astype(bf16)

    total_wait(sg.at[0, pl.ds(0, (nt - 1) * rows), :], sg_r)
    partner = h + 1 - 2 * c_half
    fwd = pltpu.make_async_remote_copy(
        sg.at[c_half], sg.at[c_half], fwd_s, fwd_r, device_id=(t, partner), device_id_type=MESH
    )
    fwd.start()
    head_wait(wt, wt_r)
    head_wait(pair_r, pb_r)
    for i in range(8, 13):
        locals_[i].wait()
    fwd.wait_recv()
    flat_ta = ta.reshape(nh * nt, prow, packs * awidth).at[pl.ds(0, nh * nt - 1)]
    total_wait(flat_ta, ta_r)

    own = single[...].astype(f32)
    full = jnp.concatenate([sg[0], sg[1]], axis=1).astype(f32)
    at_lane = iota((1, packs * awidth), 1)

    def spread(x):
        x = x.astype(f32)
        return [
            jnp.where((at_lane >= i * awidth) & (at_lane < (i + 1) * awidth), x, 0.0)
            for i in range(packs)
        ]

    lhs = jnp.concatenate(
        [
            jnp.concatenate([m.reshape(nt, 1, prow, packs * awidth) for m in spread(ta[p].astype(f32).reshape(nt * prow, packs * awidth))], axis=1)
            .reshape(nt * rows, packs * awidth)
            .astype(bf16)
            for p in range(nh)
        ],
        axis=1,
    )
    own_lhs = jnp.concatenate(
        [jnp.concatenate(spread(ta[p, t]), axis=0).astype(bf16) for p in range(nh)], axis=1
    )
    wide = jnp.concatenate([wt[p] for p in range(nh) for i in range(packs)], axis=0)
    term = dot(lhs, wide)
    own_term = dot(own_lhs, wide)
    state = own + own_term
    normed_own = layer_norm(state, gain1[...].reshape(1, width)).astype(bf16)
    normed = layer_norm(full + term, gain1[...].reshape(1, width)).astype(bf16)
    q = dot_t(normed_own, w_proj[0])
    k = dot_t(normed, w_proj[1]).astype(bf16)
    v = dot_t(normed, w_proj[2]).astype(bf16)
    gate = jax.nn.sigmoid(dot_t(normed_own, w_proj[3]))
    col = iota((1, lw), 1)
    in_head = [(col >= hd * i) & (col < hd * (i + 1)) for i in range(local_heads)]
    stacked = jnp.concatenate([jnp.where(m, q, 0.0) for m in in_head], axis=0).astype(bf16)
    s = dot_t(stacked, k) * hd ** (-0.5)
    bias = jnp.concatenate(
        [pair_r[p].astype(f32).reshape(local_heads * rows, kblock) for p in range(nh)], axis=1
    )
    s = s + bias
    e = jnp.exp(s - jnp.max(s, axis=-1, keepdims=True))
    p_ = (e / jnp.sum(e, axis=-1, keepdims=True)).astype(bf16)
    ctx = dot(p_, v)
    context = jnp.zeros((rows, lw), f32)
    for i, m in enumerate(in_head):
        context = jnp.where(m, ctx[i * rows : (i + 1) * rows], context)
    gated = (context * gate).astype(bf16)
    parts[h] = dot(gated, w_out[...]).astype(bf16)
    head_send(lambda peer: parts.at[h], parts, part_s, part_r)

    up.wait_send()
    down.wait_send()
    fwd.wait_send()
    head_wait(wt, wt_s)
    head_wait(pair_r, pb_s)
    total_wait(sg.at[0, pl.ds(0, (nt - 1) * rows), :], sg_s)
    total_wait(flat_ta, ta_s)

    head_wait(parts, part_r)
    total = parts[0].astype(f32)
    for p in range(1, nh):
        total += parts[p].astype(f32)
    after = state + total
    normed_after = layer_norm(after, gain2[...].reshape(1, width)).astype(bf16)
    g = dot(normed_after, w_gate[...])
    u = dot(normed_after, w_up[...])
    hidden = (jax.nn.silu(g) * u).astype(bf16)
    update = dot(hidden, w_down[...])
    quarter = width // nh
    for p in range(nh):
        fin_s_buf[p] = update[:, p * quarter : (p + 1) * quarter].astype(bf16)
    head_send(lambda peer: fin_s_buf.at[peer], fin_r_buf, fin_s, fin_r)
    for p in range(nh):
        own_buf[p] = after[:, p * quarter : (p + 1) * quarter]
    acc = own_buf[h] + fin_s_buf[h].astype(f32)
    fin_r_buf[h] = jnp.zeros((rows, quarter), bf16)
    head_wait(parts, part_s)
    head_wait(fin_r_buf, fin_s)
    head_wait(fin_r_buf, fin_r)
    for p in range(nh):
        acc += fin_r_buf[p].astype(f32)
    refined[...] = acc.astype(bf16)


def deliver(refined_in, mix_in, refined, atom_mix, sem):
    copies = [
        pltpu.make_async_copy(refined_in, refined, sem.at[0]),
        pltpu.make_async_copy(mix_in, atom_mix, sem.at[1]),
    ]
    for copy in copies:
        copy.start()
    for copy in copies:
        copy.wait()


def shards(
    nt,
    nh,
    single,
    pair,
    atoms,
    atom_counts,
    w_atom,
    w_atom_token,
    ln_gain,
    w_proj,
    w_pair_bias,
    w_out,
    ln_gain2,
    w_trans,
    w_trans_out,
):
    rows, width = single.shape
    slots, channels = atoms.shape
    awidth = w_atom.shape[2]
    heads = w_pair_bias.shape[1]
    local_heads = heads // nh
    kblock = pair.shape[1]
    n = nt * nh
    lw = w_proj.shape[2]
    hidden = w_trans.shape[2]
    quarter = width // nh
    vm = pl.BlockSpec(memory_space=pltpu.VMEM)
    hbm = pl.BlockSpec(memory_space=pltpu.HBM)
    dma = pltpu.SemaphoreType.DMA
    vmem = pltpu.VMEM
    refined, atom_mix = pl.pallas_call(
        functools.partial(kernel, nt, nh),
        out_shape=(vmem((rows, quarter), bf16), vmem((awidth, slots), bf16)),
        in_specs=[hbm] * 13,
        out_specs=(vm, vm),
        scratch_shapes=[
            vmem((1, rows), jnp.int32),
            vmem(single.shape, bf16),
            vmem(atoms.shape, bf16),
            vmem((3, awidth, channels), bf16),
            vmem(w_atom_token.shape, bf16),
            vmem(ln_gain.shape, bf16),
            vmem(ln_gain2.shape, bf16),
            vmem((heads, pair.shape[2]), bf16),
            vmem(pair.shape, bf16),
            vmem((4, lw, width), bf16),
            vmem(w_out.shape, bf16),
            vmem(w_trans.shape, bf16),
            vmem((width, hidden), bf16),
            vmem((width, hidden), bf16),
            vmem(w_trans_out.shape, bf16),
            dma((13,)),
            vmem((TAIL, channels), bf16),
            vmem((KWIN, channels), bf16),
            dma((2,)),
            dma((2,)),
            vmem((2, nt * rows, width // 2), bf16),
            dma,
            dma,
            dma,
            dma,
            vmem((nh, awidth, width), bf16),
            dma,
            dma,
            vmem((heads, rows, kblock), f32),
            vmem((nh, local_heads, rows, kblock), bf16),
            vmem((nh, local_heads, rows, kblock), bf16),
            dma,
            dma,
            vmem((slots, awidth), bf16),
            vmem((TAIL + slots + LEAD, awidth), bf16),
            vmem((TAIL + slots + LEAD, KWIN), bf16),
            vmem((slots, KWIN), f32),
            vmem((slots, awidth), bf16),
            vmem((nh, nt, rows * awidth // KWIN, KWIN), bf16),
            dma,
            dma,
            vmem((nh, rows, width), bf16),
            dma,
            dma,
            vmem((nh, rows, quarter), bf16),
            vmem((nh, rows, quarter), bf16),
            vmem((nh, rows, quarter), f32),
            dma,
            dma,
        ],
        compiler_params=pltpu.CompilerParams(
            collective_id=0, has_side_effects=True, vmem_limit_bytes=VMEM_MIB * 1024 * 1024
        ),
        name="step",
    )(
        single,
        pair,
        atoms,
        atom_counts.reshape(1, rows),
        jnp.transpose(w_atom, (1, 2, 0)),
        w_atom_token,
        ln_gain,
        jnp.transpose(w_proj, (1, 2, 0)),
        w_pair_bias.T,
        w_out,
        ln_gain2,
        w_trans,
        w_trans_out,
    )
    return pl.pallas_call(
        deliver,
        out_shape=(
            jax.ShapeDtypeStruct((rows, quarter), bf16),
            jax.ShapeDtypeStruct((awidth, slots), bf16),
        ),
        in_specs=[vm, vm],
        out_specs=(hbm, hbm),
        scratch_shapes=[dma((2,))],
        name="deliver",
    )(
        pltpu.with_memory_space_constraint(refined, pltpu.VMEM),
        pltpu.with_memory_space_constraint(atom_mix, pltpu.VMEM),
    )


def solution(mesh):
    return jax.shard_map(
        functools.partial(shards, mesh.shape["tok"], mesh.shape["head"]),
        mesh=mesh,
        in_specs=(
            P("tok", None),
            P("tok", "head", None),
            P("tok", None),
            P("tok"),
            P(None, None, "head"),
            P("head", None),
            P(),
            P(None, None, "head"),
            P(),
            P("head", None),
            P(),
            P(None, None, "head"),
            P("head", None),
        ),
        out_specs=(P("tok", "head"), P("head", "tok")),
        check_vma=False,
    )
```

time: 36.4 us -> 26.7 us (0.73)
  local copies, waits for them, and re-layouts: 5.18 us -> 0 us
  Pallas kernels: 30.3 us -> 25.9 us
    unnamed x3 -> x0, local copies, waits for them, and re-layouts: 5.18 us -> none
    pallas_call x1 -> x2, Pallas kernels: 30.3 us -> 25.9 us  [the longest x1 25.2 us: shards(): pl.pallas_call(functools.partial(kernel, nt, nh), out_shape=(vmem((rows,...]
where the time goes in v1:
time: 26.7 us; the launch traced here: 26.5 us
  Pallas kernels  25.9 us (97%)
  between operations  0.64 us (2%)
    pallas_call x1, Pallas kernels, shards(): pl.pallas_call(functools.partial(kernel, nt, nh), out_shape=(vmem((rows,...  25.2 us
    pallas_call x1, Pallas kernels, shards(): pl.pallas_call(deliver, out_shape=(jax.ShapeDtypeStruct((rows, quarter),...  0.65 us

profile of v1, /device:TPU:0, one launch (start us, length us, event | category | flops | bytes accessed | tf_op | source)
XLA Modules:
  0.0 26.5 jit_solution(9617897207430695191)
XLA Ops:
  0.6 25.2 %step.1 = (bf16[32,192]{1,0:T(8,128)(2,1)S(1)}, bf16[32,768]{1,0:T(8,128)(2,1)S(1)}) custom-call(bf16[32,768]{1,0:T(8,128)(2,1)} %single_hbm.1, bf16[32,64,128]{2,1,0:T(8,128)(2,1)} %pair_hbm.1, bf16[768,128]{1,0:T(8,128)(2,1)} %atoms_hbm.1, s32[1,32]{1,0:T(1,128)} %bitcast.7, bf16[3,32,128]{2,1,0:T(8,128)(2,1)} %bitcast.5, bf16[32,768]{1,0:T(8,128)(2,1)} %w_tok_hbm.1, ...), custom_call_target="tpu_custom_call" | custom-call | tf_op jit(solution)/shard_map/step/pallas_call | solution.py:522
  25.9 0.6 %deliver.1 = (bf16[32,192]{1,0:T(8,128)(2,1)}, bf16[32,768]{1,0:T(8,128)(2,1)}) custom-call(bf16[32,192]{1,0:T(8,128)(2,1)S(1)} %get-tuple-element.4.refined_in, bf16[32,768]{1,0:T(8,128)(2,1)S(1)} %get-tuple-element.5.mix_in), custom_call_target="tpu_custom_call" | custom-call | tf_op jit(solution)/shard_map/deliver/pallas_call | solution.py:597

commit v2 on v1

--- a/solution.py
+++ b/solution.py
@@ -160,20 +160,20 @@
     barrier = pltpu.get_barrier_semaphore()
     head_peers = [lax.rem(h + o, nh) for o in range(nh)]
 
-    def everyone(act):
-        for peer in head_peers[1:]:
-            act(t, peer)
-
+    def everyone(act, sign):
         def step(o, c):
-            other = lax.rem(t + o, nt)
+            other = lax.rem(t + sign * o + nt, nt)
             for peer in head_peers:
                 act(other, peer)
             return c
 
         lax.fori_loop(1, nt, step, 0)
+        for peer in head_peers[1:]:
+            act(t, peer)
 
     everyone(
-        lambda pt, ph: pl.semaphore_signal(barrier, inc=1, device_id=(pt, ph), device_id_type=MESH)
+        lambda pt, ph: pl.semaphore_signal(barrier, inc=1, device_id=(pt, ph), device_id_type=MESH),
+        -1,
     )
 
     locals_ = [
@@ -204,10 +204,40 @@
     live = jnp.sum(cnt_row, axis=1, keepdims=True).astype(jnp.int32)
     locals_[0].wait()
 
-    @pl.when(t < nt - 1)
+    has_next = t < nt - 1
+    has_prev = t > 0
+
+    @pl.when(has_next)
     def _():
         pick = iota((TAIL, slots), 1) == iota((TAIL, slots), 0) + (live - TAIL)
         tail[...] = dot(pick.astype(bf16), atoms[...]).astype(bf16)
+
+    pl.semaphore_wait(barrier, nt * nh - 1)
+
+    nxt = lax.rem(t + 1, nt)
+    prv = lax.rem(t + nt - 1, nt)
+    up = pltpu.make_async_remote_copy(
+        tail, halo.at[pl.ds(0, TAIL)], halo_s.at[0], halo_r.at[0], device_id=(nxt, h), device_id_type=MESH
+    )
+    down = pltpu.make_async_remote_copy(
+        atoms_hbm.at[pl.ds(0, LEAD)],
+        halo.at[pl.ds(TAIL, LEAD)],
+        halo_s.at[1],
+        halo_r.at[1],
+        device_id=(prv, h),
+        device_id_type=MESH,
+    )
+    pl.when(has_next)(up.start)
+    pl.when(has_prev)(down.start)
+
+    @pl.when(jnp.logical_not(has_prev))
+    def _():
+        halo[0:TAIL] = jnp.zeros((TAIL, halo.shape[1]), bf16)
+
+    @pl.when(jnp.logical_not(has_next))
+    def _():
+        halo[TAIL:] = jnp.zeros((LEAD, halo.shape[1]), bf16)
+
 
     c_half = lax.rem(h, 2)
     locals_[3].wait()
@@ -217,24 +247,6 @@
     ]
     wt[h] = w_tok[...]
 
-    pl.semaphore_wait(barrier, nt * nh - 1)
-
-    nxt = lax.rem(t + 1, nt)
-    prv = lax.rem(t + nt - 1, nt)
-    up = pltpu.make_async_remote_copy(
-        tail, halo.at[pl.ds(0, TAIL)], halo_s.at[0], halo_r.at[0], device_id=(nxt, h), device_id_type=MESH
-    )
-    down = pltpu.make_async_remote_copy(
-        atoms.at[pl.ds(0, LEAD)],
-        halo.at[pl.ds(TAIL, LEAD)],
-        halo_s.at[1],
-        halo_r.at[1],
-        device_id=(prv, h),
-        device_id_type=MESH,
-    )
-    down.start()
-    up.start()
-
     def head_send(src_of, dst, s, r):
         for peer in head_peers[1:]:
             pltpu.make_async_remote_copy(
@@ -253,7 +265,6 @@
         ).start()
         return c
 
-    lax.fori_loop(1, nt, start_sg, 0)
     head_send(lambda peer: wt.at[h], wt, wt_s, wt_r)
 
     ri = iota((rows, rows), 0)
@@ -273,15 +284,6 @@
         ref[0:TAIL, :awidth] = jnp.zeros((TAIL, awidth), bf16)
         ref[TAIL + slots :, :awidth] = jnp.zeros((LEAD, awidth), bf16)
     values[:, awidth:] = jnp.ones((values.shape[0], values.shape[1] - awidth), bf16)
-
-    locals_[5].wait()
-    locals_[6].wait()
-    for i in range(rows):
-        pair_f[:, i, :] = dot_t(w_pair[...], pair[i])
-    for p in range(nh):
-        pair_s[p] = pair_f[p * local_heads : (p + 1) * local_heads].astype(bf16)
-    pair_r[h] = pair_s[h]
-    head_send(lambda peer: pair_s.at[peer], pair_r, pb_s, pb_r)
 
     scale = awidth ** (-0.5)
     qrows = GROUP * QWIN
@@ -302,6 +304,7 @@
         inner[a : a + qrows] = jnp.where(wide_lane < 2 * awidth, pv, top)
         mixed[a : a + qrows] = (pv[:, :awidth] / pv[:, awidth : awidth + 1]).astype(bf16)
 
+    lax.fori_loop(1, nt, start_sg, 0)
     slot = iota((rows, slots), 1)
     member = (slot >= start_i) & (slot < end_i)
     inside = member & (slot >= FRONT) & ((slot < r0) | (slot >= r0 + EDGE * QWIN))
@@ -314,34 +317,24 @@
     nrow = FRONT + EDGE * QWIN
     qi = iota((nrow, KWIN), 0)
     ki = iota((nrow, KWIN), 1)
-    seen_prev = (qi < FRONT) & (ki < TAIL) & (ki >= qi // QWIN * QWIN) & (t > 0)
+    seen_prev = (qi < FRONT) & (ki < TAIL) & (ki >= qi // QWIN * QWIN) & has_prev
     reach = (qi - FRONT) // QWIN * QWIN + r0 + LEAD - live
-    seen_next = (qi >= FRONT) & (ki >= TAIL) & (ki - TAIL < reach) & (t < nt - 1)
+    seen_next = (qi >= FRONT) & (ki >= TAIL) & (ki - TAIL < reach) & has_next
     edge_mask = jnp.where(seen_prev | seen_next, 0.0, masked_value)
     pick = iota((EDGE * QWIN, slots), 1) == iota((EDGE * QWIN, slots), 0) + r0
     a_edge = dot(pick.astype(bf16), atoms[...]).astype(bf16)
     a_edge = jnp.concatenate([atoms[0:FRONT], a_edge], axis=0)
     q_edge = dot_t(a_edge, w_atom[0]).astype(bf16)
+    q_edge = dot(q_edge, w_atom[1]).astype(bf16)
     in_edge = jnp.dot(pick.astype(f32), inner[...], precision=lax.Precision.HIGHEST, preferred_element_type=f32)
     in_edge = jnp.concatenate([inner[0:FRONT], in_edge], axis=0)
     top_in = in_edge[:, 2 * awidth : 2 * awidth + 1]
 
-    locals_[7].wait()
-    woven = w_raw[...].reshape(2 * width, hidden_width)
-    blk = 128
-    si = iota((blk, 2 * blk), 0)
-    sj = iota((blk, 2 * blk), 1)
-    picks = [(sj == 2 * si + p).astype(bf16) for p in (0, 1)]
-    for b in range(width // blk):
-        for p, ref in enumerate((w_gate, w_up)):
-            ref[b * blk : (b + 1) * blk] = dot(picks[p], woven[2 * b * blk : 2 * (b + 1) * blk]).astype(bf16)
-
-    up.wait_recv()
-    down.wait_recv()
-    kh = dot_t(halo[...], w_atom[1]).astype(bf16)
+    pl.when(has_prev)(up.wait_recv)
+    pl.when(has_next)(down.wait_recv)
     vh = dot_t(halo[...], w_atom[2]).astype(bf16)
     vh = jnp.concatenate([vh, jnp.ones((KWIN, KWIN - awidth), bf16)], axis=1)
-    s = dot_t(q_edge, kh) * scale + edge_mask
+    s = dot_t(q_edge, halo[...]) * scale + edge_mask
     top_out = jnp.max(s, axis=-1, keepdims=True)
     e = jnp.exp(s - top_out).astype(bf16)
     pv = dot(e, vh)
@@ -360,7 +353,26 @@
             block, block, ta_s, ta_r, device_id=(pt, ph), device_id_type=MESH
         ).start()
 
-    everyone(ta_send)
+    everyone(ta_send, 1)
+
+    locals_[5].wait()
+    locals_[6].wait()
+    for i in range(rows):
+        pair_f[:, i, :] = dot_t(w_pair[...], pair[i])
+    for p in range(nh):
+        pair_s[p] = pair_f[p * local_heads : (p + 1) * local_heads].astype(bf16)
+    pair_r[h] = pair_s[h]
+    head_send(lambda peer: pair_s.at[peer], pair_r, pb_s, pb_r)
+
+    locals_[7].wait()
+    woven = w_raw[...].reshape(2 * width, hidden_width)
+    blk = 128
+    si = iota((blk, 2 * blk), 0)
+    sj = iota((blk, 2 * blk), 1)
+    picks = [(sj == 2 * si + p).astype(bf16) for p in (0, 1)]
+    for b in range(width // blk):
+        for p, ref in enumerate((w_gate, w_up)):
+            ref[b * blk : (b + 1) * blk] = dot(picks[p], woven[2 * b * blk : 2 * (b + 1) * blk]).astype(bf16)
 
     at_window = iota((QWIN, awidth), 0) // QWIN
     for w in range(slots // QWIN):
@@ -443,8 +455,8 @@
     parts[h] = dot(gated, w_out[...]).astype(bf16)
     head_send(lambda peer: parts.at[h], parts, part_s, part_r)
 
-    up.wait_send()
-    down.wait_send()
+    pl.when(has_next)(up.wait_send)
+    pl.when(has_prev)(down.wait_send)
     fwd.wait_send()
     head_wait(wt, wt_s)
     head_wait(pair_r, pb_s)

time: 26.7 us -> 25.7 us (0.963)
  Pallas kernels: 25.9 us -> 24.9 us
    pallas_call x1, Pallas kernels: 25.2 us -> 24.2 us  [shards(): pl.pallas_call(functools.partial(kernel, nt, nh), out_shape=(vmem((rows,...]
where the time goes in v2:
time: 25.7 us; the launch traced here: 25.5 us
  Pallas kernels  24.9 us (97%)
  between operations  0.64 us (2%)
    pallas_call x1, Pallas kernels, shards(): pl.pallas_call(functools.partial(kernel, nt, nh), out_shape=(vmem((rows,...  24.2 us
    pallas_call x1, Pallas kernels, shards(): pl.pallas_call(deliver, out_shape=(jax.ShapeDtypeStruct((rows, quarter),...  0.65 us

profile of v2, /device:TPU:0, one launch (start us, length us, event | category | flops | bytes accessed | tf_op | source)
XLA Modules:
  0.0 25.5 jit_solution(1263213582428243967)
XLA Ops:
  0.6 24.2 %step.1 = (bf16[32,192]{1,0:T(8,128)(2,1)S(1)}, bf16[32,768]{1,0:T(8,128)(2,1)S(1)}) custom-call(bf16[32,768]{1,0:T(8,128)(2,1)} %single_hbm.1, bf16[32,64,128]{2,1,0:T(8,128)(2,1)} %pair_hbm.1, bf16[768,128]{1,0:T(8,128)(2,1)} %atoms_hbm.1, s32[1,32]{1,0:T(1,128)} %bitcast.7, bf16[3,32,128]{2,1,0:T(8,128)(2,1)} %bitcast.5, bf16[32,768]{1,0:T(8,128)(2,1)} %w_tok_hbm.1, ...), custom_call_target="tpu_custom_call" | custom-call | tf_op jit(solution)/shard_map/step/pallas_call | solution.py:534
  24.9 0.6 %deliver.1 = (bf16[32,192]{1,0:T(8,128)(2,1)}, bf16[32,768]{1,0:T(8,128)(2,1)}) custom-call(bf16[32,192]{1,0:T(8,128)(2,1)S(1)} %get-tuple-element.4.refined_in, bf16[32,768]{1,0:T(8,128)(2,1)S(1)} %get-tuple-element.5.mix_in), custom_call_target="tpu_custom_call" | custom-call | tf_op jit(solution)/shard_map/deliver/pallas_call | solution.py:609

commit v3 on v2

--- a/solution.py
+++ b/solution.py
@@ -110,6 +110,7 @@
     w_up,
     w_down,
     local_sem,
+    relay,
     tail,
     halo,
     halo_s,
@@ -160,21 +161,40 @@
     barrier = pltpu.get_barrier_semaphore()
     head_peers = [lax.rem(h + o, nh) for o in range(nh)]
 
-    def everyone(act, sign):
+    has_next = t < nt - 1
+    has_prev = t > 0
+    below = t >= 2
+    above = t + 2 < nt
+    mate = t + 1 - 2 * lax.rem(t, 2)
+    cross = t + 2 * lax.rem(t, 2) - 1
+    has_cross = (cross >= 0) & (cross < nt)
+    upper = t + 4 >= nt
+    middle = jnp.logical_not(upper) & below
+    lower = jnp.logical_not(upper) & jnp.logical_not(below)
+
+    def tell(sem, pt, ph):
+        pl.semaphore_signal(sem, inc=1, device_id=(pt, ph), device_id_type=MESH)
+
+    tell(barrier, mate, h)
+    pl.when(has_cross)(lambda: tell(barrier, cross, h))
+    pl.when(below)(lambda: tell(barrier, t - 2, h))
+    pl.when(above)(lambda: tell(barrier, t + 2, h))
+    for peer in head_peers[1:]:
+        tell(barrier, t, peer)
+        tell(barrier, mate, peer)
+
+    def other(o):
+        return o + (o - t + nt) // nt
+
+    def everyone(act):
         def step(o, c):
-            other = lax.rem(t + sign * o + nt, nt)
             for peer in head_peers:
-                act(other, peer)
+                act(other(o), peer)
             return c
 
-        lax.fori_loop(1, nt, step, 0)
+        lax.fori_loop(0, nt - 1, step, 0)
         for peer in head_peers[1:]:
             act(t, peer)
-
-    everyone(
-        lambda pt, ph: pl.semaphore_signal(barrier, inc=1, device_id=(pt, ph), device_id_type=MESH),
-        -1,
-    )
 
     locals_ = [
         pltpu.make_async_copy(src, dst, local_sem.at[i])
@@ -204,15 +224,15 @@
     live = jnp.sum(cnt_row, axis=1, keepdims=True).astype(jnp.int32)
     locals_[0].wait()
 
-    has_next = t < nt - 1
-    has_prev = t > 0
-
     @pl.when(has_next)
     def _():
         pick = iota((TAIL, slots), 1) == iota((TAIL, slots), 0) + (live - TAIL)
         tail[...] = dot(pick.astype(bf16), atoms[...]).astype(bf16)
 
-    pl.semaphore_wait(barrier, nt * nh - 1)
+    some_below = (t + nt - 2) // nt
+    some_above = (2 * nt - 3 - t) // nt
+    some_cross = ((t + nt - 1) // nt) * ((2 * nt - 2 - t) // nt)
+    pl.semaphore_wait(barrier, 2 * nh - 1 + some_cross + some_below + some_above)
 
     nxt = lax.rem(t + 1, nt)
     prv = lax.rem(t + nt - 1, nt)
@@ -239,6 +259,18 @@
         halo[TAIL:] = jnp.zeros((LEAD, halo.shape[1]), bf16)
 
 
+    from_below, from_above = relay.at[0], relay.at[1]
+    pl.when(jnp.logical_not(below) & above)(lambda: tell(from_below, t + 2, h))
+    pl.when(jnp.logical_not(above) & below)(lambda: tell(from_above, t - 2, h))
+    pl.when(below)(lambda: pl.semaphore_wait(from_below, 1))
+    pl.when(below & above)(lambda: tell(from_below, t + 2, h))
+
+    def hear_above():
+        pl.semaphore_wait(from_above, 1)
+        pl.when(below)(lambda: tell(from_above, t - 2, h))
+
+    pl.when(upper & above)(hear_above)
+
     c_half = lax.rem(h, 2)
     locals_[3].wait()
     locals_[4].wait()
@@ -261,11 +293,15 @@
     def start_sg(o, c):
         block = sg.at[c_half, own_rows, :]
         pltpu.make_async_remote_copy(
-            block, block, sg_s, sg_r, device_id=(lax.rem(t + o, nt), h), device_id_type=MESH
+            block, block, sg_s, sg_r, device_id=(other(o), h), device_id_type=MESH
         ).start()
         return c
 
+    def send_single():
+        lax.fori_loop(0, nt - 1, start_sg, 0)
+
     head_send(lambda peer: wt.at[h], wt, wt_s, wt_r)
+    pl.when(upper)(send_single)
 
     ri = iota((rows, rows), 0)
     ci = iota((rows, rows), 1)
@@ -304,7 +340,6 @@
         inner[a : a + qrows] = jnp.where(wide_lane < 2 * awidth, pv, top)
         mixed[a : a + qrows] = (pv[:, :awidth] / pv[:, awidth : awidth + 1]).astype(bf16)
 
-    lax.fori_loop(1, nt, start_sg, 0)
     slot = iota((rows, slots), 1)
     member = (slot >= start_i) & (slot < end_i)
     inside = member & (slot >= FRONT) & ((slot < r0) | (slot >= r0 + EDGE * QWIN))
@@ -330,6 +365,8 @@
     in_edge = jnp.concatenate([inner[0:FRONT], in_edge], axis=0)
     top_in = in_edge[:, 2 * awidth : 2 * awidth + 1]
 
+    pl.when(middle)(hear_above)
+    pl.when(middle)(send_single)
     pl.when(has_prev)(up.wait_recv)
     pl.when(has_next)(down.wait_recv)
     vh = dot_t(halo[...], w_atom[2]).astype(bf16)
@@ -353,7 +390,9 @@
             block, block, ta_s, ta_r, device_id=(pt, ph), device_id_type=MESH
         ).start()
 
-    everyone(ta_send, 1)
+    pl.when(lower)(hear_above)
+    everyone(ta_send)
+    pl.when(lower)(send_single)
 
     locals_[5].wait()
     locals_[6].wait()
@@ -553,6 +592,7 @@
             vmem((width, hidden), bf16),
             vmem(w_trans_out.shape, bf16),
             dma((13,)),
+            pltpu.SemaphoreType.REGULAR((2,)),
             vmem((TAIL, channels), bf16),
             vmem((KWIN, channels), bf16),
             dma((2,)),

time: 25.7 us -> 24.7 us (0.961)
  Pallas kernels: 24.9 us -> 23.9 us
    pallas_call x1, Pallas kernels: 24.2 us -> 23.3 us  [shards(): pl.pallas_call(functools.partial(kernel, nt, nh), out_shape=(vmem((rows,...]
where the time goes in v3:
time: 24.7 us; the launch traced here: 24.6 us
  Pallas kernels  23.9 us (97%)
  between operations  0.64 us (3%)
    pallas_call x1, Pallas kernels, shards(): pl.pallas_call(functools.partial(kernel, nt, nh), out_shape=(vmem((rows,...  23.3 us
    pallas_call x1, Pallas kernels, shards(): pl.pallas_call(deliver, out_shape=(jax.ShapeDtypeStruct((rows, quarter),...  0.65 us

profile of v3, /device:TPU:0, one launch (start us, length us, event | category | flops | bytes accessed | tf_op | source)
XLA Modules:
  0.0 24.6 jit_solution(6734806451474581638)
XLA Ops:
  0.6 23.3 %step.1 = (bf16[32,192]{1,0:T(8,128)(2,1)S(1)}, bf16[32,768]{1,0:T(8,128)(2,1)S(1)}) custom-call(bf16[32,768]{1,0:T(8,128)(2,1)} %single_hbm.1, bf16[32,64,128]{2,1,0:T(8,128)(2,1)} %pair_hbm.1, bf16[768,128]{1,0:T(8,128)(2,1)} %atoms_hbm.1, s32[1,32]{1,0:T(1,128)} %bitcast.7, bf16[3,32,128]{2,1,0:T(8,128)(2,1)} %bitcast.5, bf16[32,768]{1,0:T(8,128)(2,1)} %w_tok_hbm.1, ...), custom_call_target="tpu_custom_call" | custom-call | tf_op jit(solution)/shard_map/step/pallas_call | solution.py:573
  23.9 0.6 %deliver.1 = (bf16[32,192]{1,0:T(8,128)(2,1)}, bf16[32,768]{1,0:T(8,128)(2,1)}) custom-call(bf16[32,192]{1,0:T(8,128)(2,1)S(1)} %get-tuple-element.4.refined_in, bf16[32,768]{1,0:T(8,128)(2,1)S(1)} %get-tuple-element.5.mix_in), custom_call_target="tpu_custom_call" | custom-call | tf_op jit(solution)/shard_map/deliver/pallas_call | solution.py:649

commit v4 on v3

--- a/solution.py
+++ b/solution.py
@@ -104,7 +104,6 @@
     w_pair,
     pair,
     w_proj,
-    w_out,
     w_raw,
     w_gate,
     w_up,
@@ -133,12 +132,19 @@
     values,
     inner,
     mixed,
+    atoms_in,
+    state_in,
+    normed_all,
+    bias,
     ta,
     ta_s,
     ta_r,
-    parts,
-    part_s,
-    part_r,
+    wo,
+    wo_s,
+    wo_r,
+    gat,
+    gat_s,
+    gat_r,
     fin_s_buf,
     fin_r_buf,
     own_buf,
@@ -167,7 +173,6 @@
     above = t + 2 < nt
     mate = t + 1 - 2 * lax.rem(t, 2)
     cross = t + 2 * lax.rem(t, 2) - 1
-    has_cross = (cross >= 0) & (cross < nt)
     upper = t + 4 >= nt
     middle = jnp.logical_not(upper) & below
     lower = jnp.logical_not(upper) & jnp.logical_not(below)
@@ -176,12 +181,18 @@
         pl.semaphore_signal(sem, inc=1, device_id=(pt, ph), device_id_type=MESH)
 
     tell(barrier, mate, h)
-    pl.when(has_cross)(lambda: tell(barrier, cross, h))
+    pl.when(below & (cross < t))(lambda: tell(barrier, cross, h))
     pl.when(below)(lambda: tell(barrier, t - 2, h))
-    pl.when(above)(lambda: tell(barrier, t + 2, h))
     for peer in head_peers[1:]:
         tell(barrier, t, peer)
         tell(barrier, mate, peer)
+
+    def tell_later(o, c):
+        for peer in head_peers:
+            tell(barrier, o, peer)
+        return c
+
+    lax.fori_loop(2 * (t // 2) + 2, nt, tell_later, 0)
 
     def other(o):
         return o + (o - t + nt) // nt
@@ -210,7 +221,7 @@
                 (w_trans_hbm, w_raw),
                 (w_proj_hbm, w_proj),
                 (gain1_hbm, gain1),
-                (w_out_hbm, w_out),
+                (w_out_hbm, wo.at[h]),
                 (gain2_hbm, gain2),
                 (w_down_hbm, w_down),
             ]
@@ -229,10 +240,10 @@
         pick = iota((TAIL, slots), 1) == iota((TAIL, slots), 0) + (live - TAIL)
         tail[...] = dot(pick.astype(bf16), atoms[...]).astype(bf16)
 
-    some_below = (t + nt - 2) // nt
+    earlier = (t // 2) * 2 * nh
     some_above = (2 * nt - 3 - t) // nt
-    some_cross = ((t + nt - 1) // nt) * ((2 * nt - 2 - t) // nt)
-    pl.semaphore_wait(barrier, 2 * nh - 1 + some_cross + some_below + some_above)
+    some_cross = lax.rem(t, 2) * ((2 * nt - 2 - t) // nt)
+    pl.semaphore_wait(barrier, earlier + 2 * nh - 1 + some_cross + some_above)
 
     nxt = lax.rem(t + 1, nt)
     prv = lax.rem(t + nt - 1, nt)
@@ -259,17 +270,11 @@
         halo[TAIL:] = jnp.zeros((LEAD, halo.shape[1]), bf16)
 
 
-    from_below, from_above = relay.at[0], relay.at[1]
-    pl.when(jnp.logical_not(below) & above)(lambda: tell(from_below, t + 2, h))
-    pl.when(jnp.logical_not(above) & below)(lambda: tell(from_above, t - 2, h))
-    pl.when(below)(lambda: pl.semaphore_wait(from_below, 1))
-    pl.when(below & above)(lambda: tell(from_below, t + 2, h))
+    pl.when(jnp.logical_not(above) & below)(lambda: tell(relay, t - 2, h))
 
     def hear_above():
-        pl.semaphore_wait(from_above, 1)
-        pl.when(below)(lambda: tell(from_above, t - 2, h))
-
-    pl.when(upper & above)(hear_above)
+        pl.semaphore_wait(relay, 1)
+        pl.when(below)(lambda: tell(relay, t - 2, h))
 
     c_half = lax.rem(h, 2)
     locals_[3].wait()
@@ -301,7 +306,25 @@
         lax.fori_loop(0, nt - 1, start_sg, 0)
 
     head_send(lambda peer: wt.at[h], wt, wt_s, wt_r)
-    pl.when(upper)(send_single)
+
+    partner = h + 1 - 2 * c_half
+    across = [lax.rem(h + o, nh) for o in range(2, nh, 2)]
+    first_part = lw // 4 // 16 * 16
+
+    def give(ref, peer, s, r):
+        return pltpu.make_async_remote_copy(ref, ref, s, r, device_id=(t, peer), device_id_type=MESH)
+
+    def give_rows(start, size):
+        for peer in across:
+            give(wo.at[h, pl.ds(start, size)], peer, wo_s.at[1], wo_r.at[1]).start()
+
+
+    def give_first():
+        locals_[10].wait()
+        give_rows(0, first_part)
+
+    pl.when(jnp.logical_not(upper))(give_first)
+    pl.when(upper & jnp.logical_not(above))(send_single)
 
     ri = iota((rows, rows), 0)
     ci = iota((rows, rows), 1)
@@ -340,6 +363,8 @@
         inner[a : a + qrows] = jnp.where(wide_lane < 2 * awidth, pv, top)
         mixed[a : a + qrows] = (pv[:, :awidth] / pv[:, awidth : awidth + 1]).astype(bf16)
 
+    pl.when(upper & above)(hear_above)
+    pl.when(upper & above)(send_single)
     slot = iota((rows, slots), 1)
     member = (slot >= start_i) & (slot < end_i)
     inside = member & (slot >= FRONT) & ((slot < r0) | (slot >= r0 + EDGE * QWIN))
@@ -364,6 +389,15 @@
     in_edge = jnp.dot(pick.astype(f32), inner[...], precision=lax.Precision.HIGHEST, preferred_element_type=f32)
     in_edge = jnp.concatenate([inner[0:FRONT], in_edge], axis=0)
     top_in = in_edge[:, 2 * awidth : 2 * awidth + 1]
+
+    locals_[5].wait()
+    locals_[6].wait()
+    for i in range(rows):
+        pair_f[:, i, :] = dot_t(w_pair[...], pair[i])
+    for p in range(nh):
+        pair_s[p] = pair_f[p * local_heads : (p + 1) * local_heads].astype(bf16)
+    pair_r[h] = pair_s[h]
+    head_send(lambda peer: pair_s.at[peer], pair_r, pb_s, pb_r)
 
     pl.when(middle)(hear_above)
     pl.when(middle)(send_single)
@@ -394,15 +428,6 @@
     everyone(ta_send)
     pl.when(lower)(send_single)
 
-    locals_[5].wait()
-    locals_[6].wait()
-    for i in range(rows):
-        pair_f[:, i, :] = dot_t(w_pair[...], pair[i])
-    for p in range(nh):
-        pair_s[p] = pair_f[p * local_heads : (p + 1) * local_heads].astype(bf16)
-    pair_r[h] = pair_s[h]
-    head_send(lambda peer: pair_s.at[peer], pair_r, pb_s, pb_r)
-
     locals_[7].wait()
     woven = w_raw[...].reshape(2 * width, hidden_width)
     blk = 128
@@ -429,70 +454,72 @@
     mix = jnp.where(alive, mixed[...].astype(f32), 0.0).astype(bf16)
     atom_mix[...] = dot_t(eye(awidth), mix).astype(bf16)
 
+    pl.when(upper)(give_first)
+    give(wo.at[h], partner, wo_s.at[0], wo_r.at[0]).start()
+    give_rows(first_part, lw - first_part)
     total_wait(sg.at[0, pl.ds(0, (nt - 1) * rows), :], sg_r)
-    partner = h + 1 - 2 * c_half
     fwd = pltpu.make_async_remote_copy(
         sg.at[c_half], sg.at[c_half], fwd_s, fwd_r, device_id=(t, partner), device_id_type=MESH
     )
     fwd.start()
     head_wait(wt, wt_r)
     head_wait(pair_r, pb_r)
-    for i in range(8, 13):
+    for i in (8, 9, 11, 12):
         locals_[i].wait()
+    bias[...] = jnp.concatenate(
+        [pair_r[p].astype(f32).reshape(local_heads * rows, kblock) for p in range(nh)], axis=1
+    )
     fwd.wait_recv()
+    for i in range(2):
+        state_in[:, i * half : (i + 1) * half] = sg[i].astype(f32)
     flat_ta = ta.reshape(nh * nt, prow, packs * awidth).at[pl.ds(0, nh * nt - 1)]
     total_wait(flat_ta, ta_r)
 
-    own = single[...].astype(f32)
-    full = jnp.concatenate([sg[0], sg[1]], axis=1).astype(f32)
     at_lane = iota((1, packs * awidth), 1)
-
-    def spread(x):
-        x = x.astype(f32)
-        return [
-            jnp.where((at_lane >= i * awidth) & (at_lane < (i + 1) * awidth), x, 0.0)
-            for i in range(packs)
-        ]
-
-    lhs = jnp.concatenate(
-        [
-            jnp.concatenate([m.reshape(nt, 1, prow, packs * awidth) for m in spread(ta[p].astype(f32).reshape(nt * prow, packs * awidth))], axis=1)
-            .reshape(nt * rows, packs * awidth)
-            .astype(bf16)
-            for p in range(nh)
-        ],
-        axis=1,
-    )
-    own_lhs = jnp.concatenate(
-        [jnp.concatenate(spread(ta[p, t]), axis=0).astype(bf16) for p in range(nh)], axis=1
-    )
-    wide = jnp.concatenate([wt[p] for p in range(nh) for i in range(packs)], axis=0)
-    term = dot(lhs, wide)
-    own_term = dot(own_lhs, wide)
-    state = own + own_term
-    normed_own = layer_norm(state, gain1[...].reshape(1, width)).astype(bf16)
-    normed = layer_norm(full + term, gain1[...].reshape(1, width)).astype(bf16)
+    blocks = [ta[p].astype(f32).reshape(nt * prow, packs * awidth) for p in range(nh)]
+    turned = []
+    for i in range(packs):
+        block = blocks[0]
+        for p in range(nh):
+            moved = blocks[p]
+            if p != i:
+                moved = pltpu.roll(moved, (p - i) % packs * awidth, axis=1)
+            block = moved if p == 0 else jnp.where(at_lane >= p * awidth, moved, block)
+        turned.append(block.reshape(nt, 1, prow, packs * awidth))
+    lhs = jnp.concatenate(turned, axis=1).reshape(nt * rows, packs * awidth).astype(bf16)
+    atoms_in[...] = lhs
+    w_full = wt[...].reshape(nh * awidth, width)
+    normed_all[...] = layer_norm(state_in[...] + dot(lhs, w_full), gain1[...].reshape(1, width)).astype(bf16)
+    normed_own = normed_all[own_rows, :]
     q = dot_t(normed_own, w_proj[0])
-    k = dot_t(normed, w_proj[1]).astype(bf16)
-    v = dot_t(normed, w_proj[2]).astype(bf16)
-    gate = jax.nn.sigmoid(dot_t(normed_own, w_proj[3]))
+    k = dot_t(normed_all[...], w_proj[1]).astype(bf16)
     col = iota((1, lw), 1)
     in_head = [(col >= hd * i) & (col < hd * (i + 1)) for i in range(local_heads)]
     stacked = jnp.concatenate([jnp.where(m, q, 0.0) for m in in_head], axis=0).astype(bf16)
     s = dot_t(stacked, k) * hd ** (-0.5)
-    bias = jnp.concatenate(
-        [pair_r[p].astype(f32).reshape(local_heads * rows, kblock) for p in range(nh)], axis=1
-    )
-    s = s + bias
+    v = dot_t(normed_all[...], w_proj[2]).astype(bf16)
+    gate = jax.nn.sigmoid(dot_t(normed_own, w_proj[3]))
+    s = s + bias[...]
     e = jnp.exp(s - jnp.max(s, axis=-1, keepdims=True))
-    p_ = (e / jnp.sum(e, axis=-1, keepdims=True)).astype(bf16)
-    ctx = dot(p_, v)
+    ctx = dot(e.astype(bf16), v) / jnp.sum(e, axis=-1, keepdims=True)
     context = jnp.zeros((rows, lw), f32)
     for i, m in enumerate(in_head):
         context = jnp.where(m, ctx[i * rows : (i + 1) * rows], context)
     gated = (context * gate).astype(bf16)
-    parts[h] = dot(gated, w_out[...]).astype(bf16)
-    head_send(lambda peer: parts.at[h], parts, part_s, part_r)
+    gat[h] = gated
+    for peer in across:
+        for far in (peer, peer + 1 - 2 * c_half):
+            give(gat.at[h], far, gat_s.at[1], gat_r.at[1]).start()
+    give(gat.at[h], partner, gat_s.at[0], gat_r.at[0]).start()
+    state = single[...].astype(f32) + dot(atoms_in[own_rows, :], wt[...].reshape(nh * awidth, width))
+    n_across = len(across)
+    total_wait(wo.at[pl.ds(0, n_across)], wo_r.at[1])
+    for peer in across:
+        give(wo.at[peer], partner, wo_s.at[2], wo_r.at[2]).start()
+    after = state + dot(gated, wo[h])
+    total_wait(wo.at[0], wo_r.at[0])
+    total_wait(gat.at[0], gat_r.at[0])
+    after += dot(gat[partner], wo[partner])
 
     pl.when(has_next)(up.wait_send)
     pl.when(has_prev)(down.wait_send)
@@ -502,11 +529,13 @@
     total_wait(sg.at[0, pl.ds(0, (nt - 1) * rows), :], sg_s)
     total_wait(flat_ta, ta_s)
 
-    head_wait(parts, part_r)
-    total = parts[0].astype(f32)
-    for p in range(1, nh):
-        total += parts[p].astype(f32)
-    after = state + total
+    total_wait(wo.at[0], wo_s.at[0])
+    total_wait(wo.at[pl.ds(0, n_across)], wo_s.at[1])
+    total_wait(wo.at[pl.ds(0, n_across)], wo_r.at[2])
+    total_wait(gat.at[pl.ds(0, 2 * n_across)], gat_r.at[1])
+    for peer in across:
+        for far in (peer, peer + 1 - 2 * c_half):
+            after += dot(gat[far], wo[far])
     normed_after = layer_norm(after, gain2[...].reshape(1, width)).astype(bf16)
     g = dot(normed_after, w_gate[...])
     u = dot(normed_after, w_up[...])
@@ -520,7 +549,9 @@
         own_buf[p] = after[:, p * quarter : (p + 1) * quarter]
     acc = own_buf[h] + fin_s_buf[h].astype(f32)
     fin_r_buf[h] = jnp.zeros((rows, quarter), bf16)
-    head_wait(parts, part_s)
+    total_wait(gat.at[0], gat_s.at[0])
+    total_wait(gat.at[pl.ds(0, 2 * n_across)], gat_s.at[1])
+    total_wait(wo.at[pl.ds(0, n_across)], wo_s.at[2])
     head_wait(fin_r_buf, fin_s)
     head_wait(fin_r_buf, fin_r)
     for p in range(nh):
@@ -586,13 +617,12 @@
             vmem((heads, pair.shape[2]), bf16),
             vmem(pair.shape, bf16),
             vmem((4, lw, width), bf16),
-            vmem(w_out.shape, bf16),
             vmem(w_trans.shape, bf16),
             vmem((width, hidden), bf16),
             vmem((width, hidden), bf16),
             vmem(w_trans_out.shape, bf16),
             dma((13,)),
-            pltpu.SemaphoreType.REGULAR((2,)),
+            pltpu.SemaphoreType.REGULAR,
             vmem((TAIL, channels), bf16),
             vmem((KWIN, channels), bf16),
             dma((2,)),
@@ -615,12 +645,19 @@
             vmem((TAIL + slots + LEAD, KWIN), bf16),
             vmem((slots, KWIN), f32),
             vmem((slots, awidth), bf16),
+            vmem((nt * rows, nh * awidth), bf16),
+            vmem((nt * rows, width), f32),
+            vmem((nt * rows, width), bf16),
+            vmem((local_heads * rows, nh * kblock), f32),
             vmem((nh, nt, rows * awidth // KWIN, KWIN), bf16),
             dma,
             dma,
-            vmem((nh, rows, width), bf16),
-            dma,
-            dma,
+            vmem((nh, lw, width), bf16),
+            dma((3,)),
+            dma((3,)),
+            vmem((nh, rows, lw), bf16),
+            dma((2,)),
+            dma((2,)),
             vmem((nh, rows, quarter), bf16),
             vmem((nh, rows, quarter), bf16),
             vmem((nh, rows, quarter), f32),

time: 24.7 us -> 23.8 us (0.964)
  Pallas kernels: 23.9 us -> 23 us
    pallas_call x1, Pallas kernels: 23.3 us -> 22.3 us  [shards(): pl.pallas_call(functools.partial(kernel, nt, nh), out_shape=(vmem((rows,...]
where the time goes in v4:
time: 23.8 us; the launch traced here: 23.6 us
  Pallas kernels  23 us (97%)
  between operations  0.64 us (3%)
    pallas_call x1, Pallas kernels, shards(): pl.pallas_call(functools.partial(kernel, nt, nh), out_shape=(vmem((rows,...  22.3 us
    pallas_call x1, Pallas kernels, shards(): pl.pallas_call(deliver, out_shape=(jax.ShapeDtypeStruct((rows, quarter),...  0.65 us

profile of v4, /device:TPU:0, one launch (start us, length us, event | category | flops | bytes accessed | tf_op | source)
XLA Modules:
  0.0 23.6 jit_solution(7320591827023305671)
XLA Ops:
  0.6 22.3 %step.1 = (bf16[32,192]{1,0:T(8,128)(2,1)S(1)}, bf16[32,768]{1,0:T(8,128)(2,1)S(1)}) custom-call(bf16[32,768]{1,0:T(8,128)(2,1)} %single_hbm.1, bf16[32,64,128]{2,1,0:T(8,128)(2,1)} %pair_hbm.1, bf16[768,128]{1,0:T(8,128)(2,1)} %atoms_hbm.1, s32[1,32]{1,0:T(1,128)} %bitcast.7, bf16[3,32,128]{2,1,0:T(8,128)(2,1)} %bitcast.5, bf16[32,768]{1,0:T(8,128)(2,1)} %w_tok_hbm.1, ...), custom_call_target="tpu_custom_call" | custom-call | tf_op jit(solution)/shard_map/step/pallas_call | solution.py:604
  23.0 0.6 %deliver.1 = (bf16[32,192]{1,0:T(8,128)(2,1)}, bf16[32,768]{1,0:T(8,128)(2,1)}) custom-call(bf16[32,192]{1,0:T(8,128)(2,1)S(1)} %get-tuple-element.4.refined_in, bf16[32,768]{1,0:T(8,128)(2,1)S(1)} %get-tuple-element.5.mix_in), custom_call_target="tpu_custom_call" | custom-call | tf_op jit(solution)/shard_map/deliver/pallas_call | solution.py:686

commit v5 on v4

--- a/solution.py
+++ b/solution.py
@@ -251,7 +251,7 @@
         tail, halo.at[pl.ds(0, TAIL)], halo_s.at[0], halo_r.at[0], device_id=(nxt, h), device_id_type=MESH
     )
     down = pltpu.make_async_remote_copy(
-        atoms_hbm.at[pl.ds(0, LEAD)],
+        atoms.at[pl.ds(0, LEAD)],
         halo.at[pl.ds(TAIL, LEAD)],
         halo_s.at[1],
         halo_r.at[1],
@@ -302,9 +302,12 @@
         ).start()
         return c
 
+    known = 2 * (t // 2) + 1
+
     def send_single():
-        lax.fori_loop(0, nt - 1, start_sg, 0)
-
+        lax.fori_loop(known, nt - 1, start_sg, 0)
+
+    lax.fori_loop(0, known, start_sg, 0)
     head_send(lambda peer: wt.at[h], wt, wt_s, wt_r)
 
     partner = h + 1 - 2 * c_half
@@ -324,7 +327,6 @@
         give_rows(0, first_part)
 
     pl.when(jnp.logical_not(upper))(give_first)
-    pl.when(upper & jnp.logical_not(above))(send_single)
 
     ri = iota((rows, rows), 0)
     ci = iota((rows, rows), 1)

time: 23.8 us -> 23.1 us (0.971)
  Pallas kernels: 23 us -> 22.3 us
    pallas_call x1, Pallas kernels: 22.3 us -> 21.7 us  [shards(): pl.pallas_call(functools.partial(kernel, nt, nh), out_shape=(vmem((rows,...]
where the time goes in v5:
time: 23.1 us; the launch traced here: 23 us
  Pallas kernels  22.3 us (97%)
  between operations  0.64 us (3%)
    pallas_call x1, Pallas kernels, shards(): pl.pallas_call(functools.partial(kernel, nt, nh), out_shape=(vmem((rows,...  21.7 us
    pallas_call x1, Pallas kernels, shards(): pl.pallas_call(deliver, out_shape=(jax.ShapeDtypeStruct((rows, quarter),...  0.65 us

profile of v5, /device:TPU:0, one launch (start us, length us, event | category | flops | bytes accessed | tf_op | source)
XLA Modules:
  0.0 23.0 jit_solution(1038619243164369529)
XLA Ops:
  0.6 21.7 %step.1 = (bf16[32,192]{1,0:T(8,128)(2,1)S(1)}, bf16[32,768]{1,0:T(8,128)(2,1)S(1)}) custom-call(bf16[32,768]{1,0:T(8,128)(2,1)} %single_hbm.1, bf16[32,64,128]{2,1,0:T(8,128)(2,1)} %pair_hbm.1, bf16[768,128]{1,0:T(8,128)(2,1)} %atoms_hbm.1, s32[1,32]{1,0:T(1,128)} %bitcast.7, bf16[3,32,128]{2,1,0:T(8,128)(2,1)} %bitcast.5, bf16[32,768]{1,0:T(8,128)(2,1)} %w_tok_hbm.1, ...), custom_call_target="tpu_custom_call" | custom-call | tf_op jit(solution)/shard_map/step/pallas_call | solution.py:606
  22.3 0.6 %deliver.1 = (bf16[32,192]{1,0:T(8,128)(2,1)}, bf16[32,768]{1,0:T(8,128)(2,1)}) custom-call(bf16[32,192]{1,0:T(8,128)(2,1)S(1)} %get-tuple-element.4.refined_in, bf16[32,768]{1,0:T(8,128)(2,1)S(1)} %get-tuple-element.5.mix_in), custom_call_target="tpu_custom_call" | custom-call | tf_op jit(solution)/shard_map/deliver/pallas_call | solution.py:688

commit v6 on v5

--- a/solution.py
+++ b/solution.py
@@ -387,7 +387,6 @@
     a_edge = dot(pick.astype(bf16), atoms[...]).astype(bf16)
     a_edge = jnp.concatenate([atoms[0:FRONT], a_edge], axis=0)
     q_edge = dot_t(a_edge, w_atom[0]).astype(bf16)
-    q_edge = dot(q_edge, w_atom[1]).astype(bf16)
     in_edge = jnp.dot(pick.astype(f32), inner[...], precision=lax.Precision.HIGHEST, preferred_element_type=f32)
     in_edge = jnp.concatenate([inner[0:FRONT], in_edge], axis=0)
     top_in = in_edge[:, 2 * awidth : 2 * awidth + 1]
@@ -405,9 +404,10 @@
     pl.when(middle)(send_single)
     pl.when(has_prev)(up.wait_recv)
     pl.when(has_next)(down.wait_recv)
+    kh = dot_t(halo[...], w_atom[1]).astype(bf16)
     vh = dot_t(halo[...], w_atom[2]).astype(bf16)
     vh = jnp.concatenate([vh, jnp.ones((KWIN, KWIN - awidth), bf16)], axis=1)
-    s = dot_t(q_edge, halo[...]) * scale + edge_mask
+    s = dot_t(q_edge, kh) * scale + edge_mask
     top_out = jnp.max(s, axis=-1, keepdims=True)
     e = jnp.exp(s - top_out).astype(bf16)
     pv = dot(e, vh)

time: 23.1 us -> 23.2 us (level)
  no operation moved by 1% of the time
where the time goes in v6:
time: 23.2 us; the launch traced here: 23.1 us
  Pallas kernels  22.4 us (97%)
  between operations  0.64 us (3%)
    pallas_call x1, Pallas kernels, shards(): pl.pallas_call(functools.partial(kernel, nt, nh), out_shape=(vmem((rows,...  21.8 us
    pallas_call x1, Pallas kernels, shards(): pl.pallas_call(deliver, out_shape=(jax.ShapeDtypeStruct((rows, quarter),...  0.65 us

profile of v6, /device:TPU:0, one launch (start us, length us, event | category | flops | bytes accessed | tf_op | source)
XLA Modules:
  0.0 23.1 jit_solution(6617243896790991645)
XLA Ops:
  0.6 21.8 %step.1 = (bf16[32,192]{1,0:T(8,128)(2,1)S(1)}, bf16[32,768]{1,0:T(8,128)(2,1)S(1)}) custom-call(bf16[32,768]{1,0:T(8,128)(2,1)} %single_hbm.1, bf16[32,64,128]{2,1,0:T(8,128)(2,1)} %pair_hbm.1, bf16[768,128]{1,0:T(8,128)(2,1)} %atoms_hbm.1, s32[1,32]{1,0:T(1,128)} %bitcast.7, bf16[3,32,128]{2,1,0:T(8,128)(2,1)} %bitcast.5, bf16[32,768]{1,0:T(8,128)(2,1)} %w_tok_hbm.1, ...), custom_call_target="tpu_custom_call" | custom-call | tf_op jit(solution)/shard_map/step/pallas_call | solution.py:606
  22.4 0.6 %deliver.1 = (bf16[32,192]{1,0:T(8,128)(2,1)}, bf16[32,768]{1,0:T(8,128)(2,1)}) custom-call(bf16[32,192]{1,0:T(8,128)(2,1)S(1)} %get-tuple-element.4.refined_in, bf16[32,768]{1,0:T(8,128)(2,1)S(1)} %get-tuple-element.5.mix_in), custom_call_target="tpu_custom_call" | custom-call | tf_op jit(solution)/shard_map/deliver/pallas_call | solution.py:688
